TPU v7x, 32 devices: a whole 2x2x4 slice. The times are simulated.
32 devices in a mesh: group: 2 (over y), branch: 4 (over x, core), tensor: 4 (over z).
Axes of the slice: x: 2, y: 2, z: 4, core: 2. Of those that a mesh axis runs over, the one named last changes fastest.
Arguments:
- queries: bfloat16 [2048, 8192], P(('group', 'branch'), 'tensor'), parts along dimension 0, may hold values from -160 to 160
- prefix_cache: bfloat16 [2, 3072, 1024], P(None, 'group', 'tensor'), parts along dimension 1, may hold values from -5 to 5
- prior_cache: bfloat16 [2, 2048, 1024], P(None, ('group', 'branch'), 'tensor'), parts along dimension 1, may hold values from -5 to 5
- fresh_cache: bfloat16 [2, 2048, 1024], P(None, ('group', 'branch'), 'tensor'), parts along dimension 1, may hold values from -5 to 5
- visible: int32 [8, 4], P('group'), parts along dimension 0, may hold values 0 or 1
- turn_order: int32 [8], P('group'), parts along dimension 0, may hold values from 0 to 3, each once
- output_weight: bfloat16 [8192, 8192], P('tensor', 'branch'), may hold values from -0.0625 to 0.0625
Outputs:
- projected: bfloat16 [2048, 8192], P(('group', 'branch'), 'tensor'), parts along dimension 0
There are 2 independent parts, one for each index of `group`. A program takes and returns all parts, laid end to end along the dimension named above; an argument that names none is the same for every part. Nothing has to cross between parts.
Inputs may be any that keep to these rules, and one draw needn't show every extreme that they name: `turn_order`: each of 0 to 3 once.
All inputs are finite; a program needn't handle non-finite values.
Results may differ from a plain program's by a relative error of at most 0.015.
Values may be sent and summed in bfloat16 or wider, within the bound.
No kernel may reach another device: no remote copies, remote signals or barrier semaphores. Data moves between devices by JAX's collectives and lax.ppermute only.
A program may use at most 64 MiB of HBM per device.

v0:
```python
import math

import jax
import jax.numpy as jnp
from jax import lax
from jax.sharding import PartitionSpec as P

HD = 128


NEGATIVE = -1e30


def largest_divisor(total_rows, ceiling):
    chosen = 1
    for candidate in range(1, min(total_rows, ceiling) + 1):
        if total_rows % candidate == 0:
            chosen = candidate
    return chosen


def update_state(running, query_heads, key_rows, value_rows, allowed):
    peak_old, total_old, summed_old = running
    scores = jnp.einsum(
        "qhgd,khd->hgqk", query_heads, key_rows, preferred_element_type=jnp.float32
    ) / math.sqrt(HD)
    if allowed is None:
        masked = scores
    else:
        masked = jnp.where(allowed, scores, NEGATIVE)
    peak_new = jnp.maximum(peak_old, jnp.max(masked, axis=-1))
    weights = jnp.exp(masked - peak_new[..., None])
    if allowed is not None:
        weights = jnp.where(allowed, weights, 0.0)
    factor = jnp.exp(peak_old - peak_new)
    total_new = total_old * factor + jnp.sum(weights, axis=-1)
    summed_new = summed_old * factor[..., None] + jnp.einsum(
        "hgqk,khd->hgqd",
        weights.astype(jnp.bfloat16),
        value_rows,
        preferred_element_type=jnp.float32,
    )
    return (peak_new, total_new, summed_new)


def sweep(running, query_heads, key_rows, value_rows, allow_rows):
    row_count = key_rows.shape[0]
    block_rows = largest_divisor(row_count, 1024)
    if block_rows == row_count:
        return update_state(running, query_heads, key_rows, value_rows, allow_rows(0, row_count))
    block_count = row_count // block_rows
    key_blocks = key_rows.reshape(block_count, block_rows, key_rows.shape[1], key_rows.shape[2])
    value_blocks = value_rows.reshape(
        block_count, block_rows, value_rows.shape[1], value_rows.shape[2]
    )

    def advance(state, inputs):
        key_block, value_block, position = inputs
        return (
            update_state(
                state,
                query_heads,
                key_block,
                value_block,
                allow_rows(position * block_rows, block_rows),
            ),
            None,
        )

    running, unused = lax.scan(
        advance, running, (key_blocks, value_blocks, jnp.arange(block_count, dtype=jnp.int32))
    )
    return running


def per_device(queries, prefix_cache, prior_cache, fresh_cache, visible, turn_order, output_weight):
    message_rows = queries.shape[0]
    local_heads = queries.shape[1] // HD
    local_groups = prefix_cache.shape[2] // HD
    sharing = local_heads // local_groups
    query_heads = queries.reshape(message_rows, local_groups, sharing, HD)
    agent_index = lax.axis_index("branch")
    agent_count = visible.shape[0]
    seen_row = lax.dynamic_slice_in_dim(visible, agent_index, 1, 0)[0]
    own_turn = lax.dynamic_slice_in_dim(turn_order, agent_index, 1, 0)[0]
    positions = jnp.arange(message_rows, dtype=jnp.int32)
    agent_ids = jnp.arange(agent_count, dtype=jnp.int32)

    def split_cache(cache):
        return (cache[0].reshape(-1, local_groups, HD), cache[1].reshape(-1, local_groups, HD))

    def whole_rows(offset, count):
        return None

    start_state = (
        jnp.full((local_groups, sharing, message_rows), NEGATIVE, jnp.float32),
        jnp.zeros((local_groups, sharing, message_rows), jnp.float32),
        jnp.zeros((local_groups, sharing, message_rows, HD), jnp.float32),
    )
    prefix_keys, prefix_values = split_cache(prefix_cache)
    prefix_state = sweep(start_state, query_heads, prefix_keys, prefix_values, whole_rows)

    def add_messages(running, pieces, root):
        prior_keys, prior_values = split_cache(pieces[0])
        fresh_keys, fresh_values = split_cache(pieces[1])

        def locate(offset, count):
            row_index = root + offset + jnp.arange(count, dtype=jnp.int32)
            owner_ids = row_index // message_rows
            onehot = owner_ids[:, None] == agent_ids[None, :]
            return (row_index, owner_ids, onehot)

        def prior_allowed(offset, count):
            row_index, owner_ids, onehot = locate(offset, count)
            visible_rows = jnp.sum(jnp.where(onehot, seen_row[None, :], 0), axis=1) > 0
            return visible_rows[None, :]

        def fresh_allowed(offset, count):
            row_index, owner_ids, onehot = locate(offset, count)
            turn_values = jnp.sum(jnp.where(onehot, turn_order[None, :], 0), axis=1)
            earlier = turn_values < own_turn
            causal = (owner_ids == agent_index)[None, :] & (
                (row_index % message_rows)[None, :] <= positions[:, None]
            )
            return earlier[None, :] | causal

        running = sweep(running, query_heads, prior_keys, prior_values, prior_allowed)
        return sweep(running, query_heads, fresh_keys, fresh_values, fresh_allowed)

    peak_final, total_final, summed_final = add_messages(
        prefix_state,
        (
            lax.all_gather(prior_cache, "branch", axis=1, tiled=True),
            lax.all_gather(fresh_cache, "branch", axis=1, tiled=True),
        ),
        jnp.int32(0),
    )
    heads_out = (summed_final / total_final[..., None]).astype(jnp.bfloat16)
    attention = jnp.transpose(heads_out, (2, 0, 1, 3)).reshape(message_rows, local_heads * HD)
    product = jnp.dot(
        lax.all_gather(attention, "branch", axis=0, tiled=True),
        output_weight,
        preferred_element_type=jnp.float32,
    )
    partial_columns = product.astype(jnp.bfloat16).astype(jnp.float32)
    column_totals = lax.psum_scatter(
        partial_columns.astype(jnp.bfloat16), "tensor", scatter_dimension=1, tiled=True
    )
    result = lax.all_to_all(column_totals, "branch", split_axis=0, concat_axis=1, tiled=True)
    return result


def solution(mesh):
    return jax.shard_map(
        per_device,
        mesh=mesh,
        in_specs=(
            P(("group", "branch"), "tensor"),
            P(None, "group", "tensor"),
            P(None, ("group", "branch"), "tensor"),
            P(None, ("group", "branch"), "tensor"),
            P("group", None),
            P("group"),
            P("tensor", "branch"),
        ),
        out_specs=P(("group", "branch"), "tensor"),
        check_vma=False,
    )
```

profile of v0, /device:TPU:0, one launch (start us, length us, event | category | flops | bytes accessed | tf_op | source)
XLA Modules:
  0.0 239.5 jit_solution(15426722531047207641)
XLA Ops:
  6.5 0.0 copy-start
  6.5 0.0 all-gather.4.cloned.1.call-start
  6.5 1.8 copy.35
  8.3 0.0 all-gather.4.cloned.1.call-update
  8.4 0.0 all-gather.6.cloned.1.call-start
  8.4 1.8 copy.40
  10.2 0.0 all-gather.6.cloned.1.call-update
  10.2 0.0 all-gather.8.cloned.1.call-start
  10.3 2.3 copy.31
  12.6 1.6 copy.33
  14.2 2.6 %fusion.45 = (bf16[1,1536,256]{2,1,0:T(8,128)(2,1)}, bf16[1,1536,256]{2,1,0:T(8,128)(2,1)}) fusion(bf16[2,1536,256]{2,1,0:T(8,128)(2,1)} %param.10), kind=kLoop, calls=%fused_computation.70 | loop fusion | bytes 3145728 | tf_op jit(solution)/shard_map/slice | solution.py:90
  16.8 2.7 %reshape_reshape_squeeze.7 = bf16[2,768,2,128]{3,2,1,0:T(2,128)(2,1)} reshape(bf16[1,1536,256]{2,1,0:T(8,128)(2,1)} %get-tuple-element.112) | data formatting | bytes 1572864 | tf_op jit(solution)/shard_map/reshape;reshape;squeeze | solution.py:53
  19.6 2.7 %reshape_reshape_squeeze.6 = bf16[2,768,2,128]{3,2,1,0:T(2,128)(2,1)} reshape(bf16[1,1536,256]{2,1,0:T(8,128)(2,1)} %get-tuple-element.113) | data formatting | bytes 1572864 | tf_op jit(solution)/shard_map/reshape;reshape;squeeze | solution.py:52
  22.3 0.0 copy-start.4
  22.3 18.8 %while.15 = (s32[]{:T(128)}, f32[2,8,256]{2,1,0:T(8,128)S(1)}, f32[2,8,256]{2,1,0:T(8,128)S(1)}, f32[2,8,256,128]{3,2,1,0:T(8,128)S(1)}, bf16[2,768,2,128]{3,2,1...) while((s32[]{:T(128)}, f32[2,8,256]{2,1,0:T(8,128)S(1)}, ...), condition=%wide.region_3.4_spmd.clone, body=%wide.region_0.3_spmd.clone.sunk | while | flops 1637371904 | bytes 45613172 | solution.py:70
  22.3 1.7 constant_dynamic-slice_fusion.3
  23.9 1.8 bitcast_reduce_fusion.3
  25.8 2.1 fusion.64
  27.9 3.8 %fusion.66 = f32[2,8,256,128]{3,2,1,0:T(8,128)S(1)} fusion(f32[2,8,256,128]{3,2,1,0:T(8,128)S(1)} %get-tuple-element.191, f32[2,768,256,8]{2,1,3,0:T(8,128)S(1)} %get-tuple-element.175, f32[2,8,256]{2,1,0:T(8,128)S(1)} %select_maximum_fusion.2, f32[2,8,256]{2,1,0:T(8,128)S(1)} %get-tuple-element.177, pred[]{:T(512)S(6)} %compare.10, ...), kind=kOutput, calls=%fused_computation.9.clone.1 | convolution fusion | flops 816316416 | bytes 17203200 | tf_op jit(solution)/shard_map/while/body/eval_jaxpr/hgqk,khd->hgqd/dot_general | solution.py:37
  31.7 1.7 constant_dynamic-slice_fusion.3
  33.3 1.8 bitcast_reduce_fusion.3
  35.2 2.1 fusion.64
  37.2 3.8 %fusion.66 = f32[2,8,256,128]{3,2,1,0:T(8,128)S(1)} fusion(f32[2,8,256,128]{3,2,1,0:T(8,128)S(1)} %get-tuple-element.191, f32[2,768,256,8]{2,1,3,0:T(8,128)S(1)} %get-tuple-element.175, f32[2,8,256]{2,1,0:T(8,128)S(1)} %select_maximum_fusion.2, f32[2,8,256]{2,1,0:T(8,128)S(1)} %get-tuple-element.177, pred[]{:T(512)S(6)} %compare.10, ...), kind=kOutput, calls=%fused_computation.9.clone.1 | convolution fusion | flops 816316416 | bytes 17203200 | tf_op jit(solution)/shard_map/while/body/eval_jaxpr/hgqk,khd->hgqd/dot_general | solution.py:37
  41.0 0.0 copy-done
  41.1 0.0 copy-done.4
  41.1 0.6 dynamic_slice.14
  41.6 1.8 copy.38
  43.5 0.1 select_reduce_fusion
  43.6 0.6 broadcast_compare_fusion.1
  44.2 1.0 fusion.30
  45.1 0.0 all-gather.4.cloned.1.call-done
  45.2 1.3 fusion.47
  46.4 0.0 copy-start.2
  46.4 8.6 %bitcast_reduce_fusion.1 = (f32[2,8,256]{2,1,0:T(8,128)S(1)}, f32[2,1024,256,8]{2,1,3,0:T(8,128)}) fusion(pred[1024]{0:T(1024)(128)(4,1)S(1)} %get-tuple-element.123, bf16[1024,2,128,1]{0,2,3,1:T(8,128)(2,1)S(1)} %bitcast.107, bf16[256,2,8,128]{0,3,2,1:T(8,128)(2,1)} %bitcast.104), kind=kOutput, calls=%fused_computation.22 | convolution fusion | flops 1086320640 | bytes 18367488 | tf_op jit(solution)/shard_map/qhgd,khd->hgqk/dot_general | solution.py:24
  55.0 0.0 all-gather.6.cloned.1.call-done
  55.0 1.3 fusion.46
  56.3 0.0 copy-done.2
  56.3 2.8 %fusion.15 = (f32[2,8,256]{2,1,0:T(8,128)S(1)}, f32[2,1024,256,8]{2,1,3,0:T(8,128)S(1)}) fusion(pred[256,1024]{0,1:T(8,128)(4,1)S(1)} %fusion.30, bf16[1024,2,128,1]{0,2,3,1:T(8,128)(2,1)S(1)} %bitcast.108, bf16[256,2,8,128]{0,3,2,1:T(8,128)(2,1)S(1)} %bitcast.105), kind=kOutput, calls=%fused_computation.27 | convolution fusion | flops 1086320640 | bytes 18628608 | tf_op jit(solution)/shard_map/qhgd,khd->hgqk/dot_general | solution.py:24
  59.1 8.2 %fusion.18 = f32[2,8,256]{2,1,0:T(8,128)S(1)} fusion(f32[2,1024,256,8]{2,1,3,0:T(8,128)} %get-tuple-element.121, f32[2,8,256]{2,1,0:T(8,128)S(1)} %get-tuple-element.107, pred[1024]{0:T(1024)(128)(4,1)S(1)} %get-tuple-element.123), kind=kLoop, calls=%fused_computation.30 | loop fusion | flops 20967424 | bytes 16811008 | tf_op jit(solution)/shard_map/reduce_sum | solution.py:36
  67.3 8.2 %fusion.20 = f32[2,8,256,128]{2,3,1,0:T(8,128)S(1)} fusion(bf16[1024,2,128,1]{0,2,3,1:T(8,128)(2,1)S(1)} %bitcast.112, f32[2,1024,256,8]{2,1,3,0:T(8,128)} %get-tuple-element.121, f32[2,8,256]{2,1,0:T(8,128)S(1)} %get-tuple-element.107, pred[1024]{0:T(1024)(128)(4,1)S(1)} %get-tuple-element.123), kind=kOutput, calls=%fused_computation.32 | convolution fusion | flops 1094713344 | bytes 19416064 | tf_op jit(solution)/shard_map/hgqk,khd->hgqd/dot_general | solution.py:37
  75.4 0.0 copy-start.3
  75.4 4.0 %fusion.16 = f32[2,8,256]{2,1,0:T(8,128)S(1)} fusion(f32[2,1024,256,8]{2,1,3,0:T(8,128)S(1)} %get-tuple-element.119, f32[2,8,256]{2,1,0:T(8,128)S(1)} %get-tuple-element.106, pred[256,1024]{0,1:T(8,128)(4,1)S(1)} %fusion.30), kind=kLoop, calls=%fused_computation.28 | loop fusion | flops 20967424 | bytes 17072128 | tf_op jit(solution)/shard_map/reduce_sum | solution.py:36
  79.5 0.0 copy-done.3
  79.5 5.6 %divide_convert_fusion = bf16[2,8,256,128]{2,3,1,0:T(8,128)(2,1)} fusion(f32[2,8,256,128]{2,3,1,0:T(8,128)S(1)} %fusion.20, f32[2,8,256,128]{2,3,1,0:T(8,128)S(1)} %copy-done.3, bf16[1024,2,128,1]{0,2,3,1:T(8,128)(2,1)S(1)} %bitcast.111, f32[2,1024,256,8]{2,1,3,0:T(8,128)S(1)} %get-tuple-element.119, f32[2,8,256]{2,1,0:T(8,128)S(1)} %get-tuple-element.106, ...), kind=kOutput, calls=%fused_computation.38 | convolution fusion | flops 1097859072 | bytes 22872064 | tf_op jit(solution)/shard_map/hgqk,khd->hgqd/dot_general | solution.py:37
  85.1 0.0 all-gather.8.cloned.1.call-update
  85.1 0.0 reduce-scatter.2.cloned.1.call-start
  85.1 37.8 %all-gather.8.cloned.1.call-done = bf16[1024,2048]{0,1:T(8,128)(2,1)} async-done(((bf16[256,2048]{0,1:T(8,128)(2,1)}), bf16[1024,2048]{0,1:T(8,128)(2,1)}) %all-gather.8.cloned.1.call-update) | async-done | bytes 4194320 | tf_op jit(solution)/shard_map/all_gather | solution.py:141
  123.0 0.0 copy-start.1
  123.0 14.0 %convolution_convert_fusion = bf16[1024,2048]{1,0:T(8,128)(2,1)} fusion(bf16[1024,2048]{0,1:T(8,128)(2,1)} %all-gather.8.cloned.1.call-done, bf16[2048,2048]{1,0:T(8,128)(2,1)} %param.15), kind=kOutput, calls=%fused_computation.37 | convolution fusion | flops 8592031744 | bytes 16777216 | tf_op jit(solution)/shard_map/dot_general | solution.py:140
  137.0 0.0 reduce-scatter.2.cloned.1.call-update
  137.0 77.0 %reduce-scatter.2.cloned.1.call-done = bf16[1024,512]{1,0:T(8,128)(2,1)} async-done(((bf16[1024,2048]{1,0:T(8,128)(2,1)}), bf16[1024,512]{1,0:T(8,128)(2,1)}) %reduce-scatter.2.cloned.1.call-update) | async-done | bytes 1048592 | tf_op jit(solution)/shard_map/reduce_scatter | solution.py:146
  214.0 17.9 %all_to_all.19 = bf16[4,256,512]{2,1,0:T(8,128)(2,1)S(1)} all-to-all(bf16[4,256,512]{2,1,0:T(8,128)(2,1)} %bitcast.110), channel_id=1, replica_groups=mesh['group'=2,'branch'=4,'tensor'=4] {'branch'}, dimensions={0} | all-to-all | bytes 2097152 | tf_op jit(solution)/shard_map/all_to_all | solution.py:149
  231.9 1.1 copy.62
  233.0 0.0 copy-done.1
  (15 shorter events, 0.1 us)
Async XLA Ops:
  6.5 34.5 %copy-start = (s32[4,4]{1,0:T(4,128)S(1)}, s32[4,4]{1,0:T(4,128)}, u32[]{:S(2)}) copy-start(s32[4,4]{1,0:T(4,128)} %param.13) | copy-start | bytes 196
  6.5 38.6 %all-gather.4.cloned.1.call-start = ((), (), s32[]{:S(2)}) async-start(), calls=%async_computation.2 | async-start | bytes 1310720 | tf_op jit(solution)/shard_map/all_gather | solution.py:133
  8.4 46.6 %all-gather.6.cloned.1.call-start = ((), (), s32[]{:S(2)}) async-start(), calls=%async_computation.3 | async-start | bytes 1310720 | tf_op jit(solution)/shard_map/all_gather | solution.py:134
  10.2 112.7 %all-gather.8.cloned.1.call-start = ((), (), s32[]{:S(2)}) async-start(), calls=%async_computation.4 | async-start | bytes 5242880 | tf_op jit(solution)/shard_map/all_gather | solution.py:141
  22.3 18.8 %copy-start.4 = (s32[4]{0:T(128)S(1)}, s32[4]{0:T(128)}, u32[]{:S(2)}) copy-start(s32[4]{0:T(128)} %param.14) | copy-start | bytes 52
  46.4 9.8 %copy-start.2 = (bf16[256,2048]{0,1:T(8,128)(2,1)S(1)}, bf16[256,2048]{0,1:T(8,128)(2,1)}, u32[]{:S(2)}) copy-start(bf16[256,2048]{0,1:T(8,128)(2,1)} %copy.31) | copy-start | bytes 3145732
  75.4 4.1 %copy-start.3 = (f32[2,8,256,128]{2,3,1,0:T(8,128)S(1)}, f32[2,8,256,128]{2,3,1,0:T(8,128)}, u32[]{:S(2)}) copy-start(f32[2,8,256,128]{2,3,1,0:T(8,128)} %copy.38) | copy-start | bytes 6291460
  85.1 128.9 %reduce-scatter.2.cloned.1.call-start = ((), (), s32[]{:S(2)}) async-start(), calls=%async_computation.5 | async-start | bytes 5242880 | tf_op jit(solution)/shard_map/reduce_scatter | solution.py:146
  123.0 110.0 %copy-start.1 = (s32[4,4]{1,0:T(4,128)S(1)}, s32[4,4]{1,0:T(4,128)}, u32[]{:S(2)}) copy-start(s32[4,4]{1,0:T(4,128)} %param.13) | copy-start | bytes 196
Sparse Core Ops, SparseCore 0:
  8.9 19.5 all-gather.3
  30.0 16.8 all-gather.5
  85.2 37.7 all-gather.7
  137.1 76.7 reduce-scatter.1
where the time goes:
time: 240 us
  waiting for transfers between devices  115 us (48%)
  matrix products  50.2 us (21%)
  local copies, waits for them, and re-layouts  24.9 us (10%)
  other arithmetic  18 us (8%)
  blocking collectives  17.9 us (7%)
  between operations  13.3 us (6%)
    reduce_scatter x1, waiting for transfers between devices, per_device(): lax.psum_scatter(partial_columns.astype(jnp.bfloat16), 'tensor', scatter_...  77 us
    all_gather x1, waiting for transfers between devices, per_device(): lax.all_gather(attention, 'branch', axis=0, tiled=True)  37.8 us
    dot_general x4, matrix products, update_state(): jnp.einsum('hgqk,khd->hgqd', weights.astype(jnp.bfloat16), value_rows, pr...  21.3 us
    all_to_all x1, blocking collectives, per_device(): lax.all_to_all(column_totals, 'branch', split_axis=0, concat_axis=1, tile...  17.9 us
    reduce_sum x4, other arithmetic, update_state(): total_new = total_old * factor + jnp.sum(weights, axis=-1)  16.3 us
    dot_general x4, matrix products, update_state(): jnp.einsum('qhgd,khd->hgqk', query_heads, key_rows, preferred_element_typ...  14.9 us
    dot_general x1, matrix products, per_device(): jnp.dot(lax.all_gather(attention, 'branch', axis=0, tiled=True), output_w...  14 us
    unnamed x14, local copies, waits for them, and re-layouts  7.48 us
  transfers between devices with their start and end apart: 4, of which 2 were waited for; matrix products, arithmetic and copies ran while one was open for 19% of the time, Pallas kernels for 0%

commit v1 on v0

v1 whole, which is shorter than its diff:
```python
import functools
import math

import jax
import jax.numpy as jnp
from jax import lax
from jax.experimental import pallas as pl
from jax.experimental.pallas import tpu as pltpu
from jax.sharding import PartitionSpec as P

HD = 128
NEGATIVE = -1e30
LOG2E = 1.4426950408889634

CHUNK_PARTS = (1, 1, 1, 1)


def exchange(value, axis, size, bit):
    return lax.ppermute(value, axis, [(i, i ^ bit) for i in range(size)])


def cost(flops, reads, exps=0):
    return pl.CostEstimate(
        flops=int(flops), bytes_accessed=int(reads), transcendentals=int(exps)
    )


def scores_of(rows, keys):
    return lax.dot_general(
        rows, keys, (((1,), (1,)), ((), ())), preferred_element_type=jnp.float32
    )


def widen(values):
    return jnp.concatenate([values, jnp.ones_like(values)], axis=1)


def prefix_body(query_ref, cache_ref, state_ref, *, sharing, factor):
    keys = cache_ref[0]
    values = widen(cache_ref[1])
    for head in range(sharing):
        rows = query_ref[:, head * HD : (head + 1) * HD]
        scores = scores_of(rows, keys)
        peak = jnp.max(scores, axis=-1, keepdims=True)
        weights = jnp.exp2((scores - peak) * factor).astype(jnp.bfloat16)
        both = jnp.dot(weights, values, preferred_element_type=jnp.float32)
        lane = lax.broadcasted_iota(jnp.int32, (rows.shape[0], HD), 1)
        state_ref[0, head, :, :HD] = both[:, :HD]
        state_ref[0, head, :, HD:] = jnp.where(lane < HD // 2, peak, both[:, HD:])


def prefix_attention(queries, prefix_cache, groups, sharing):
    rows = queries.shape[0]
    prefix = prefix_cache.shape[1]
    return pl.pallas_call(
        functools.partial(
            prefix_body, sharing=sharing, factor=LOG2E / math.sqrt(HD)
        ),
        grid=(groups,),
        in_specs=[
            pl.BlockSpec((rows, sharing * HD), lambda g: (0, g)),
            pl.BlockSpec((2, prefix, HD), lambda g: (0, 0, g)),
        ],
        out_specs=pl.BlockSpec((1, sharing, rows, 2 * HD), lambda g: (g, 0, 0, 0)),
        out_shape=jax.ShapeDtypeStruct((groups, sharing, rows, 2 * HD), jnp.float32),
        name="prefix",
        cost_estimate=cost(
            8 * groups * sharing * rows * prefix * HD,
            queries.size * 2 + prefix_cache.size * 2 + groups * sharing * rows * 8 * HD,
            groups * sharing * rows * prefix,
        ),
    )(queries, prefix_cache)


def message_body(
    place_ref, visible_ref, turn_ref, query_ref, state_ref, *refs, sharing, counts, offset, factor
):
    pieces = 2 * len(counts)
    caches = refs[:pieces]
    out_ref, stacked, gathered, peaks = refs[pieces:]
    rows = query_ref.shape[0]
    for head in range(sharing):
        at = slice(head * rows, (head + 1) * rows)
        stacked[at, :] = query_ref[:, head * HD : (head + 1) * HD]
        kept = state_ref[0, head]
        gathered[at, :HD] = kept[:, :HD]
        gathered[at, HD:] = jnp.broadcast_to(kept[:, 2 * HD - 1 :], (rows, HD))
        peaks[at, :] = jnp.broadcast_to(kept[:, HD : HD + 1], (rows, HD))
    me = place_ref[0]
    own_turn = turn_ref[me]

    def add_block(keys, values, causal):
        scores = scores_of(stacked[...], keys)
        if causal:
            spot = lax.broadcasted_iota(jnp.int32, scores.shape, 0) % rows + offset
            scores = jnp.where(
                lax.broadcasted_iota(jnp.int32, scores.shape, 1) <= spot, scores, NEGATIVE
            )
        before = peaks[...]
        now = jnp.maximum(before, jnp.max(scores, axis=-1, keepdims=True))
        peaks[...] = now
        wide = jnp.concatenate([now] * (keys.shape[0] // HD), axis=1)
        weights = jnp.exp2((scores - wide) * factor).astype(jnp.bfloat16)
        shrink = jnp.exp2((before - now) * factor)
        gathered[...] = gathered[...] * jnp.concatenate([shrink, shrink], axis=1) + jnp.dot(
            weights, widen(values), preferred_element_type=jnp.float32
        )

    for number, count in enumerate(counts):
        prior_ref, fresh_ref = caches[2 * number : 2 * number + 2]

        def one(index, prior_ref=prior_ref, fresh_ref=fresh_ref, number=number):
            agent = place_ref[2 + number] + index

            @pl.when(visible_ref[me, agent] == 1)
            def _():
                add_block(prior_ref[index, 0], prior_ref[index, 1], False)

            @pl.when(turn_ref[agent] < own_turn)
            def _():
                add_block(fresh_ref[index, 0], fresh_ref[index, 1], False)

            @pl.when(agent == me)
            def _():
                add_block(fresh_ref[index, 0], fresh_ref[index, 1], True)

        if count == 1:
            one(0)
        else:
            lax.fori_loop(0, count, lambda index, carry: (one(index), carry)[1], 0)

    for head in range(sharing):
        at = slice(head * rows, (head + 1) * rows)
        out_ref[:, head * HD : (head + 1) * HD] = (
            gathered[at, :HD] / gathered[at, HD:]
        ).astype(jnp.bfloat16)


def message_attention(place, visible, turn_order, queries, state, caches, rows, offset):
    groups, sharing = state.shape[0], state.shape[1]
    message = caches[0].shape[2]
    counts = tuple(cache.shape[0] for cache in caches[::2])
    agents = sum(counts)
    chunk = offset // rows
    return pl.pallas_call(
        functools.partial(
            message_body,
            sharing=sharing,
            counts=counts,
            offset=offset,
            factor=LOG2E / math.sqrt(HD),
        ),
        grid_spec=pltpu.PrefetchScalarGridSpec(
            num_scalar_prefetch=3,
            grid=(groups,),
            in_specs=[
                pl.BlockSpec((rows, sharing * HD), lambda g, *_: (chunk, g)),
                pl.BlockSpec((1, sharing, rows, 2 * HD), lambda g, *_: (g, 0, chunk, 0)),
            ]
            + [
                pl.BlockSpec((cache.shape[0], 2, message, HD), lambda g, *_: (0, 0, 0, g))
                for cache in caches
            ],
            out_specs=pl.BlockSpec((rows, sharing * HD), lambda g, *_: (0, g)),
            scratch_shapes=[
                pltpu.VMEM((sharing * rows, HD), jnp.bfloat16),
                pltpu.VMEM((sharing * rows, 2 * HD), jnp.float32),
                pltpu.VMEM((sharing * rows, HD), jnp.float32),
            ],
        ),
        out_shape=jax.ShapeDtypeStruct((rows, groups * sharing * HD), jnp.bfloat16),
        name="messages",
        cost_estimate=cost(
            8 * groups * sharing * rows * 2 * agents * message * HD,
            rows * groups * sharing * HD * 12 + agents * message * groups * HD * 8,
            groups * sharing * rows * 2 * agents * message,
        ),
    )(place, visible, turn_order, queries, state, *caches)


def project_body(columns_ref, *refs):
    *row_refs, weight_ref, out_ref = refs
    rows = jnp.concatenate([row_ref[...] for row_ref in row_refs], axis=0)
    out_ref[0] = jnp.dot(
        rows, weight_ref[...], preferred_element_type=jnp.float32
    ).astype(jnp.bfloat16)


def project(columns, pieces, output_weight, width):
    rows, depth = pieces[0].shape
    blocks = columns.shape[0]
    total = rows * len(pieces)
    return pl.pallas_call(
        project_body,
        grid_spec=pltpu.PrefetchScalarGridSpec(
            num_scalar_prefetch=1,
            grid=(blocks,),
            in_specs=[pl.BlockSpec((rows, depth), lambda j, c: (0, 0)) for piece in pieces]
            + [pl.BlockSpec((depth, width), lambda j, c: (0, c[j]))],
            out_specs=pl.BlockSpec((1, total, width), lambda j, c: (j, 0, 0)),
        ),
        out_shape=jax.ShapeDtypeStruct((blocks, total, width), jnp.bfloat16),
        name="project",
        cost_estimate=cost(
            2 * total * depth * width * blocks,
            2 * (total * depth + depth * width * blocks + total * width * blocks),
        ),
    )(columns, *pieces, output_weight)


def place_body(place_ref, *refs):
    pieces = refs[:-1] if len(refs) % 2 else refs[:-2]
    out_ref = refs[-1]
    width = pieces[0].shape[1]
    for number, piece in enumerate(pieces):
        at = pl.multiple_of((place_ref[0] ^ number) * width, width)
        out_ref[:, pl.ds(at, width)] = piece[...]


def place_columns(place, pieces, whole, message, offset):
    rows, width = pieces[0].shape
    columns = width * len(pieces)
    chunk = offset // rows
    specs = [pl.BlockSpec((rows, width), lambda i, p: (0, 0)) for piece in pieces]
    operands = list(pieces)
    aliases = {}
    if whole is not None:
        specs.append(pl.BlockSpec(memory_space=pl.ANY))
        operands.append(whole)
        aliases = {len(operands): 0}
    return pl.pallas_call(
        place_body,
        grid_spec=pltpu.PrefetchScalarGridSpec(
            num_scalar_prefetch=1,
            grid=(1,),
            in_specs=specs,
            out_specs=pl.BlockSpec((rows, columns), lambda i, p: (chunk, 0)),
        ),
        out_shape=jax.ShapeDtypeStruct((message, columns), jnp.bfloat16),
        input_output_aliases=aliases,
        name="place",
        cost_estimate=cost(0, 4 * rows * columns),
    )(place, *operands)


def spread(value, axis, size):
    pieces = {0: value}
    bit = size // 2
    while bit:
        for offset in list(pieces):
            pieces[offset | bit] = exchange(pieces[offset], axis, size, bit)
        bit //= 2
    return [pieces[offset] for offset in range(size)]


def wide(value):
    return value.astype(jnp.float32)


def finish(attention, output_weight):
    product = jnp.dot(
        lax.all_gather(attention, "branch", axis=0, tiled=True),
        output_weight,
        preferred_element_type=jnp.float32,
    )
    column_totals = lax.psum_scatter(
        product.astype(jnp.bfloat16), "tensor", scatter_dimension=1, tiled=True
    )
    return lax.all_to_all(column_totals, "branch", split_axis=0, concat_axis=1, tiled=True)


def per_device(
    branches,
    tensors,
    queries,
    prefix_cache,
    prior_cache,
    fresh_cache,
    visible,
    turn_order,
    output_weight,
):
    message = queries.shape[0]
    groups = prefix_cache.shape[2] // HD
    sharing = queries.shape[1] // HD // groups
    width = output_weight.shape[1] // tensors
    agent = lax.axis_index("branch").astype(jnp.int32)
    slot = lax.axis_index("tensor").astype(jnp.int32)
    powers = all(size & (size - 1) == 0 for size in (branches, tensors))
    chunked = powers and branches <= 4 and tensors > 1 and width % HD == 0

    if not chunked:
        caches = (
            jnp.swapaxes(lax.all_gather(prior_cache, "branch", axis=1, tiled=False), 0, 1),
            jnp.swapaxes(lax.all_gather(fresh_cache, "branch", axis=1, tiled=False), 0, 1),
        )
        place = jnp.stack([agent, slot, jnp.int32(0)])
        state = prefix_attention(queries, prefix_cache, groups, sharing)
        rows = message // 4
        attention = jnp.concatenate(
            [
                message_attention(
                    place, visible, turn_order, queries, state, caches, rows, offset
                )
                for offset in range(0, message, rows)
            ],
            axis=0,
        )
        return finish(attention, output_weight)

    others = jnp.arange(branches, dtype=jnp.int32) ^ agent
    place = jnp.concatenate([agent[None], slot[None], others])
    steps = jnp.arange(tensors, dtype=jnp.int32)
    sent_columns = slot ^ (2 * steps[: tensors // 2] + 1)
    kept_columns = slot ^ (2 * steps[: tensors // 2])

    prior = spread(prior_cache, "branch", branches)
    fresh = spread(fresh_cache, "branch", branches)
    state = prefix_attention(queries, prefix_cache, groups, sharing)
    caches = [cache[None] for pair in zip(prior, fresh) for cache in pair]

    unit = message // sum(CHUNK_PARTS)
    result = None
    offset = 0
    for part in CHUNK_PARTS:
        rows = unit * part
        attention = message_attention(
            place, visible, turn_order, queries, state, caches, rows, offset
        )
        pieces = spread(attention, "branch", branches)
        sent = project(sent_columns, pieces, output_weight, width)
        arrived = exchange(sent, "tensor", tensors, 1)
        kept = project(kept_columns, pieces, output_weight, width)
        total = wide(kept) + wide(arrived)
        bit = 2
        while bit < tensors:
            arrived = exchange(total[1::2].astype(jnp.bfloat16), "tensor", tensors, bit)
            total = total[0::2] + wide(arrived)
            bit *= 2
        summed = total[0].astype(jnp.bfloat16).reshape(branches, rows, width)
        columns = [
            exchange(summed[number], "branch", branches, number) if number else summed[0]
            for number in range(branches)
        ]
        result = place_columns(place, columns, result, message, offset)
        offset += rows
    return result


def solution(mesh):
    return jax.shard_map(
        functools.partial(per_device, mesh.shape["branch"], mesh.shape["tensor"]),
        mesh=mesh,
        in_specs=(
            P(("group", "branch"), "tensor"),
            P(None, "group", "tensor"),
            P(None, ("group", "branch"), "tensor"),
            P(None, ("group", "branch"), "tensor"),
            P("group", None),
            P("group"),
            P("tensor", "branch"),
        ),
        out_specs=P(("group", "branch"), "tensor"),
        check_vma=False,
    )
```

time: 240 us -> 189 us (0.79)
  Pallas kernels: 0 us -> 76.6 us
  waiting for transfers between devices: 115 us -> 57.2 us
  matrix products: 50.2 us -> 0 us
  starting transfers between devices: 0.13 us -> 41.8 us
  blocking collectives: 17.9 us -> 0 us
  local copies, waits for them, and re-layouts: 24.9 us -> 7.93 us
  other arithmetic: 18 us -> 3.3 us
  between operations: 13.3 us -> 0.35 us
    reduce_scatter x1 -> x0, waiting for transfers between devices: 77 us -> none  [per_device(): lax.psum_scatter(partial_columns.astype(jnp.bfloat16), 'tensor', scatter_...]
    pallas_call x0 -> x17, Pallas kernels: none -> 76.6 us  [the longest x8 37.5 us: project(): pl.pallas_call(project_body, grid_spec=pltpu.PrefetchScalarGridSpec(num_s...]
    ppermute x0 -> x38, waiting for transfers between devices: none -> 57.2 us  [exchange(): return lax.ppermute(value, axis, [(i, i ^ bit) for i in range(size)])]
    dot_general x9 -> x0, matrix products: 50.2 us -> none  [the longest x4 21.3 us: update_state(): jnp.einsum('hgqk,khd->hgqd', weights.astype(jnp.bfloat16), value_rows, pr...]
    ppermute x0 -> x38, starting transfers between devices: none -> 41.8 us  [exchange(): return lax.ppermute(value, axis, [(i, i ^ bit) for i in range(size)])]
    all_gather x3 -> x0, waiting for transfers between devices: 37.9 us -> none  [the longest x1 37.8 us: per_device(): lax.all_gather(attention, 'branch', axis=0, tiled=True)]
    all_to_all x1 -> x0, blocking collectives: 17.9 us -> none  [per_device(): lax.all_to_all(column_totals, 'branch', split_axis=0, concat_axis=1, tile...]
    reduce_sum x5 -> x0, other arithmetic: 16.4 us -> none  [the longest x4 16.3 us: update_state(): total_new = total_old * factor + jnp.sum(weights, axis=-1)]
  transfers between devices with their start and end apart: 4 -> 38, of which waited for: 2 -> 8; matrix products, arithmetic and copies ran while one was open for 19% -> 3% of each run, Pallas kernels for 0% -> 35%
where the time goes in v1:
time: 189 us; the launch traced here: 187 us
  Pallas kernels  76.6 us (41%)
  waiting for transfers between devices  57.2 us (30%)
  starting transfers between devices  41.8 us (22%)
  local copies, waits for them, and re-layouts  7.93 us (4%)
  other arithmetic  3.3 us (2%)
    ppermute x38, waiting for transfers between devices, exchange(): return lax.ppermute(value, axis, [(i, i ^ bit) for i in range(size)])  57.2 us
    ppermute x38, starting transfers between devices, exchange(): return lax.ppermute(value, axis, [(i, i ^ bit) for i in range(size)])  41.8 us
    pallas_call x8, Pallas kernels, project(): pl.pallas_call(project_body, grid_spec=pltpu.PrefetchScalarGridSpec(num_s...  37.5 us
    pallas_call x4, Pallas kernels, message_attention(): pl.pallas_call(functools.partial(message_body, sharing=sharing, counts=co...  18.8 us
    pallas_call x1, Pallas kernels, prefix_attention(): pl.pallas_call(functools.partial(prefix_body, sharing=sharing, factor=LOG...  11 us
    pallas_call x4, Pallas kernels, place_columns(): pl.pallas_call(place_body, grid_spec=pltpu.PrefetchScalarGridSpec(num_sca...  9.29 us
    unnamed x70, local copies, waits for them, and re-layouts  5.22 us
  transfers between devices with their start and end apart: 38, of which 8 were waited for; matrix products, arithmetic and copies ran while one was open for 3% of the time, Pallas kernels for 35%

profile of v1, /device:TPU:0, one launch (start us, length us, event | category | flops | bytes accessed | tf_op | source)
XLA Modules:
  0.0 187.1 jit_solution(772085730843000289)
XLA Ops:
  0.0 3.0 %collective-permute-start.2 = (bf16[2,256,256]{2,1,0:T(8,128)(2,1)}, bf16[2,256,256]{2,1,0:T(8,128)(2,1)S(1)}, u32[]{:S(2)}, u32[]{:S(2)}) collective-permute-start(bf16[2,256,256]{2,1,0:T(8,128)(2,1)} %param.9), channel_id=1, source_target_pairs={{0,8},{4,12},{8,0},{12,4},{1,9},{5,13},{9,1},{13,5},{2,10},{6,14},... | collective-permute-start | bytes 786440 | tf_op jit(solution)/shard_map/ppermute | solution.py:19
  3.0 0.5 collective-permute-start.1
  3.5 6.8 %collective-permute-done.2 = bf16[2,256,256]{2,1,0:T(8,128)(2,1)S(1)} collective-permute-done((bf16[2,256,256]{2,1,0:T(8,128)(2,1)}, bf16[2,256,256]{2,1,0:T(8,128)(2,1)S(1)}, u32[]{:S(2)}, u32[]{:S(2)}) %collective-permute-start.2) | collective-permute-done | bytes 262176 | tf_op jit(solution)/shard_map/ppermute | solution.py:19
  10.3 4.8 %collective-permute-done.3 = bf16[2,256,256]{2,1,0:T(8,128)(2,1)S(1)} collective-permute-done((bf16[2,256,256]{2,1,0:T(8,128)(2,1)}, bf16[2,256,256]{2,1,0:T(8,128)(2,1)S(1)}, u32[]{:S(2)}, u32[]{:S(2)}) %collective-permute-start.3) | collective-permute-done | bytes 262176 | tf_op jit(solution)/shard_map/ppermute | solution.py:19
  15.1 11.0 %prefix.1.state_ref = f32[2,8,256,256]{3,2,1,0:T(8,128)} custom-call(bf16[256,2048]{1,0:T(8,128)(2,1)} %query_ref.9, bf16[2,1536,256]{2,1,0:T(8,128)(2,1)} %cache_ref.1), custom_call_target="tpu_custom_call" | custom-call | flops 6442450944 | bytes 6815744 | tf_op jit(solution)/shard_map/prefix/pallas_call | solution.py:55
  26.2 0.6 pad_add_fusion.place_ref
  26.8 0.6 copy-done.31
  27.7 4.6 %messages.5.refs_0_ = bf16[64,2048]{1,0:T(8,128)(2,1)} custom-call(s32[6]{0:T(128)} %pad_add_fusion.place_ref, s32[4,4]{1,0:T(4,128)} %visible_ref.7, s32[4]{0:T(128)} %turn_ref.7, bf16[256,2048]{1,0:T(8,128)(2,1)} %query_ref.9, f32[2,8,256,256]{3,2,1,0:T(8,128)} %prefix.1.state_ref, bf16[1,2,256,256]{3,2,1,0:T(8,128)(2,1)} %bitcast.42, ...), custom_call_target="tpu_custom_call" | custom-call | flops 2147483648 | bytes 3670016 | tf_op jit(solution)/shard_map/messages/pallas_call | solution.py:145
  32.3 4.9 %messages.4.refs_0_ = bf16[64,2048]{1,0:T(8,128)(2,1)} custom-call(s32[6]{0:T(128)} %pad_add_fusion.place_ref, s32[4,4]{1,0:T(4,128)} %visible_ref.7, s32[4]{0:T(128)} %turn_ref.7, bf16[256,2048]{1,0:T(8,128)(2,1)} %query_ref.9, f32[2,8,256,256]{3,2,1,0:T(8,128)} %prefix.1.state_ref, bf16[1,2,256,256]{3,2,1,0:T(8,128)(2,1)} %bitcast.43, ...), custom_call_target="tpu_custom_call" | custom-call | flops 2147483648 | bytes 3670016 | tf_op jit(solution)/shard_map/messages/pallas_call | solution.py:145
  37.2 9.4 %collective-permute-start.7 = (bf16[64,2048]{1,0:T(8,128)(2,1)}, bf16[64,2048]{1,0:T(8,128)(2,1)S(1)}, u32[]{:S(2)}, u32[]{:S(2)}) collective-permute-start(bf16[64,2048]{1,0:T(8,128)(2,1)} %messages.4.refs_0_), channel_id=1, source_target_pairs={{0,8},{4,12},{8,0},{12,4},{1,9},{5,13},{9,1},{13,5},{2,10},{6,14},... | collective-permute-start | bytes 786440 | tf_op jit(solution)/shard_map/ppermute | solution.py:19
  46.7 0.4 collective-permute-start.15
  47.1 4.6 %messages.6.refs_0_ = bf16[64,2048]{1,0:T(8,128)(2,1)} custom-call(s32[6]{0:T(128)} %pad_add_fusion.place_ref, s32[4,4]{1,0:T(4,128)} %visible_ref.7, s32[4]{0:T(128)} %turn_ref.7, bf16[256,2048]{1,0:T(8,128)(2,1)} %query_ref.9, f32[2,8,256,256]{3,2,1,0:T(8,128)} %prefix.1.state_ref, bf16[1,2,256,256]{3,2,1,0:T(8,128)(2,1)} %bitcast.44, ...), custom_call_target="tpu_custom_call" | custom-call | flops 2147483648 | bytes 3670016 | tf_op jit(solution)/shard_map/messages/pallas_call | solution.py:145
  51.7 5.7 %collective-permute-start.23 = (bf16[64,2048]{1,0:T(8,128)(2,1)}, bf16[64,2048]{1,0:T(8,128)(2,1)S(1)}, u32[]{:S(2)}, u32[]{:S(2)}) collective-permute-start(bf16[64,2048]{1,0:T(8,128)(2,1)} %messages.6.refs_0_), channel_id=1, source_target_pairs={{0,8},{4,12},{8,0},{12,4},{1,9},{5,13},{9,1},{13,5},{2,10},{6,14},... | collective-permute-start | bytes 786440 | tf_op jit(solution)/shard_map/ppermute | solution.py:19
  57.3 4.8 %messages.7.refs_0_ = bf16[64,2048]{1,0:T(8,128)(2,1)} custom-call(s32[6]{0:T(128)} %pad_add_fusion.place_ref, s32[4,4]{1,0:T(4,128)} %visible_ref.7, s32[4]{0:T(128)} %turn_ref.7, bf16[256,2048]{1,0:T(8,128)(2,1)} %query_ref.9, f32[2,8,256,256]{3,2,1,0:T(8,128)} %prefix.1.state_ref, bf16[1,2,256,256]{3,2,1,0:T(8,128)(2,1)} %bitcast.45, ...), custom_call_target="tpu_custom_call" | custom-call | flops 2147483648 | bytes 3670016 | tf_op jit(solution)/shard_map/messages/pallas_call | solution.py:145
  62.1 3.9 %collective-permute-start.31 = (bf16[64,2048]{1,0:T(8,128)(2,1)}, bf16[64,2048]{1,0:T(8,128)(2,1)S(1)}, u32[]{:S(2)}, u32[]{:S(2)}) collective-permute-start(bf16[64,2048]{1,0:T(8,128)(2,1)} %messages.7.refs_0_), channel_id=1, source_target_pairs={{0,8},{4,12},{8,0},{12,4},{1,9},{5,13},{9,1},{13,5},{2,10},{6,14},... | collective-permute-start | bytes 786440 | tf_op jit(solution)/shard_map/ppermute | solution.py:19
  66.2 0.4 collective-permute-start.22
  66.8 0.4 collective-permute-start.24
  67.2 0.5 broadcast_xor_fusion
  67.7 5.5 %collective-permute-done.31.refs_2_ = bf16[64,2048]{1,0:T(8,128)(2,1)S(1)} collective-permute-done((bf16[64,2048]{1,0:T(8,128)(2,1)}, bf16[64,2048]{1,0:T(8,128)(2,1)S(1)}, u32[]{:S(2)}, u32[]{:S(2)}) %collective-permute-start.31) | collective-permute-done | bytes 262176 | tf_op jit(solution)/shard_map/ppermute | solution.py:19
  73.3 0.4 collective-permute-start.32
  73.7 0.3 copy-done.10
  74.0 4.7 %project.9 = bf16[2,256,512]{2,1,0:T(8,128)(2,1)} custom-call(s32[2]{0:T(128)} %get-tuple-element.22.columns_ref, bf16[64,2048]{1,0:T(8,128)(2,1)} %messages.4.refs_0_, bf16[64,2048]{1,0:T(8,128)(2,1)} %copy-done.5, bf16[64,2048]{1,0:T(8,128)(2,1)} %copy-done.3, bf16[64,2048]{1,0:T(8,128)(2,1)} %copy-done.10, bf16[2048,2048]{1,0:T(8,128)(2,1)} %refs_4_.15), custom_call_target="tpu_custom_call" | custom-call | flops 1073741824 | bytes 5767168 | tf_op jit(solution)/shard_map/project/pallas_call | solution.py:193
  78.7 1.6 collective-permute-start.9
  80.4 4.7 %project.11 = bf16[2,256,512]{2,1,0:T(8,128)(2,1)} custom-call(s32[2]{0:T(128)} %get-tuple-element.22.columns_ref, bf16[64,2048]{1,0:T(8,128)(2,1)} %messages.5.refs_0_, bf16[64,2048]{1,0:T(8,128)(2,1)} %copy-done.7, bf16[64,2048]{1,0:T(8,128)(2,1)} %copy-done.6, bf16[64,2048]{1,0:T(8,128)(2,1)} %copy-done.13, bf16[2048,2048]{1,0:T(8,128)(2,1)} %refs_4_.15), custom_call_target="tpu_custom_call" | custom-call | flops 1073741824 | bytes 5767168 | tf_op jit(solution)/shard_map/project/pallas_call | solution.py:193
  85.1 0.7 collective-permute-start.17
  85.8 0.7 copy-done.14
  86.5 4.7 %project.13 = bf16[2,256,512]{2,1,0:T(8,128)(2,1)} custom-call(s32[2]{0:T(128)} %get-tuple-element.22.columns_ref, bf16[64,2048]{1,0:T(8,128)(2,1)} %messages.6.refs_0_, bf16[64,2048]{1,0:T(8,128)(2,1)} %copy-done.12, bf16[64,2048]{1,0:T(8,128)(2,1)} %copy-done.9, bf16[64,2048]{1,0:T(8,128)(2,1)} %copy-done.14, bf16[2048,2048]{1,0:T(8,128)(2,1)} %refs_4_.15), custom_call_target="tpu_custom_call" | custom-call | flops 1073741824 | bytes 5767168 | tf_op jit(solution)/shard_map/project/pallas_call | solution.py:193
  91.1 1.4 collective-permute-start.25
  92.5 0.7 copy-done.15
  93.2 0.7 copy-done.16
  93.9 4.7 %project.15 = bf16[2,256,512]{2,1,0:T(8,128)(2,1)} custom-call(s32[2]{0:T(128)} %get-tuple-element.22.columns_ref, bf16[64,2048]{1,0:T(8,128)(2,1)} %messages.7.refs_0_, bf16[64,2048]{1,0:T(8,128)(2,1)} %copy-done.15, bf16[64,2048]{1,0:T(8,128)(2,1)} %copy-done.11, bf16[64,2048]{1,0:T(8,128)(2,1)} %copy-done.16, bf16[2048,2048]{1,0:T(8,128)(2,1)} %refs_4_.15), custom_call_target="tpu_custom_call" | custom-call | flops 1073741824 | bytes 5767168 | tf_op jit(solution)/shard_map/project/pallas_call | solution.py:193
  98.6 0.6 collective-permute-start.33
  99.2 4.7 %project.14 = bf16[2,256,512]{2,1,0:T(8,128)(2,1)} custom-call(s32[2]{0:T(128)} %get-tuple-element.21.columns_ref, bf16[64,2048]{1,0:T(8,128)(2,1)} %messages.7.refs_0_, bf16[64,2048]{1,0:T(8,128)(2,1)} %copy-done.15, bf16[64,2048]{1,0:T(8,128)(2,1)} %copy-done.11, bf16[64,2048]{1,0:T(8,128)(2,1)} %copy-done.16, bf16[2048,2048]{1,0:T(8,128)(2,1)} %refs_4_.15), custom_call_target="tpu_custom_call" | custom-call | flops 1073741824 | bytes 5767168 | tf_op jit(solution)/shard_map/project/pallas_call | solution.py:193
  103.9 4.7 %project.12 = bf16[2,256,512]{2,1,0:T(8,128)(2,1)} custom-call(s32[2]{0:T(128)} %get-tuple-element.21.columns_ref, bf16[64,2048]{1,0:T(8,128)(2,1)} %messages.6.refs_0_, bf16[64,2048]{1,0:T(8,128)(2,1)} %copy-done.12, bf16[64,2048]{1,0:T(8,128)(2,1)} %copy-done.9, bf16[64,2048]{1,0:T(8,128)(2,1)} %copy-done.14, bf16[2048,2048]{1,0:T(8,128)(2,1)} %refs_4_.15), custom_call_target="tpu_custom_call" | custom-call | flops 1073741824 | bytes 5767168 | tf_op jit(solution)/shard_map/project/pallas_call | solution.py:193
  108.6 4.7 %project.10 = bf16[2,256,512]{2,1,0:T(8,128)(2,1)} custom-call(s32[2]{0:T(128)} %get-tuple-element.21.columns_ref, bf16[64,2048]{1,0:T(8,128)(2,1)} %messages.5.refs_0_, bf16[64,2048]{1,0:T(8,128)(2,1)} %copy-done.7, bf16[64,2048]{1,0:T(8,128)(2,1)} %copy-done.6, bf16[64,2048]{1,0:T(8,128)(2,1)} %copy-done.13, bf16[2048,2048]{1,0:T(8,128)(2,1)} %refs_4_.15), custom_call_target="tpu_custom_call" | custom-call | flops 1073741824 | bytes 5767168 | tf_op jit(solution)/shard_map/project/pallas_call | solution.py:193
  113.2 4.8 %project.8 = bf16[2,256,512]{2,1,0:T(8,128)(2,1)} custom-call(s32[2]{0:T(128)} %get-tuple-element.21.columns_ref, bf16[64,2048]{1,0:T(8,128)(2,1)} %messages.4.refs_0_, bf16[64,2048]{1,0:T(8,128)(2,1)} %copy-done.5, bf16[64,2048]{1,0:T(8,128)(2,1)} %copy-done.3, bf16[64,2048]{1,0:T(8,128)(2,1)} %copy-done.10, bf16[2048,2048]{1,0:T(8,128)(2,1)} %refs_4_.15), custom_call_target="tpu_custom_call" | custom-call | flops 1073741824 | bytes 5767168 | tf_op jit(solution)/shard_map/project/pallas_call | solution.py:193
  118.1 1.4 convert_add_fusion.3
  119.5 2.6 %collective-permute-start.10 = (bf16[1,256,512]{2,1,0:T(8,128)(2,1)S(1)}, bf16[1,256,512]{2,1,0:T(8,128)(2,1)S(1)}, u32[]{:S(2)}, u32[]{:S(2)}) collective-permute-start(bf16[1,256,512]{2,1,0:T(8,128)(2,1)S(1)} %slice.259), channel_id=1, source_target_pairs={{0,2},{1,3},{2,0},{3,1},{4,6},{5,7},{6,4},{7,5},{8,10},{9,11},{10,... | collective-permute-start | bytes 786440 | tf_op jit(solution)/shard_map/ppermute | solution.py:19
  122.2 0.2 convert_add_fusion.2
  122.4 0.4 collective-permute-start.18
  122.8 0.1 convert_add_fusion.1
  123.0 2.6 %collective-permute-start.26 = (bf16[1,256,512]{2,1,0:T(8,128)(2,1)S(1)}, bf16[1,256,512]{2,1,0:T(8,128)(2,1)S(1)}, u32[]{:S(2)}, u32[]{:S(2)}) collective-permute-start(bf16[1,256,512]{2,1,0:T(8,128)(2,1)S(1)} %slice.257), channel_id=1, source_target_pairs={{0,2},{1,3},{2,0},{3,1},{4,6},{5,7},{6,4},{7,5},{8,10},{9,11},{10,... | collective-permute-start | bytes 786440 | tf_op jit(solution)/shard_map/ppermute | solution.py:19
  125.6 7.7 %collective-permute-done.33 = bf16[2,256,512]{2,1,0:T(8,128)(2,1)S(1)} collective-permute-done((bf16[2,256,512]{2,1,0:T(8,128)(2,1)}, bf16[2,256,512]{2,1,0:T(8,128)(2,1)S(1)}, u32[]{:S(2)}, u32[]{:S(2)}) %collective-permute-start.33) | collective-permute-done | bytes 524320 | tf_op jit(solution)/shard_map/ppermute | solution.py:19
  133.6 24.2 %collective-permute-done.18 = bf16[1,256,512]{2,1,0:T(8,128)(2,1)S(1)} collective-permute-done((bf16[1,256,512]{2,1,0:T(8,128)(2,1)S(1)}, bf16[1,256,512]{2,1,0:T(8,128)(2,1)S(1)}, u32[]{:S(2)}, u32[]{:S(2)}) %collective-permute-start.18) | collective-permute-done | bytes 262176 | tf_op jit(solution)/shard_map/ppermute | solution.py:19
  157.8 0.6 slice_bitcast_fusion.8
  158.5 4.9 %collective-permute-done.26 = bf16[1,256,512]{2,1,0:T(8,128)(2,1)S(1)} collective-permute-done((bf16[1,256,512]{2,1,0:T(8,128)(2,1)S(1)}, bf16[1,256,512]{2,1,0:T(8,128)(2,1)S(1)}, u32[]{:S(2)}, u32[]{:S(2)}) %collective-permute-start.26) | collective-permute-done | bytes 262176 | tf_op jit(solution)/shard_map/ppermute | solution.py:19
  163.5 0.6 slice_bitcast_fusion.4
  164.1 1.6 collective-permute-start.28
  165.7 1.9 %collective-permute-done.34 = bf16[1,256,512]{2,1,0:T(8,128)(2,1)S(1)} collective-permute-done((bf16[1,256,512]{2,1,0:T(8,128)(2,1)S(1)}, bf16[1,256,512]{2,1,0:T(8,128)(2,1)S(1)}, u32[]{:S(2)}, u32[]{:S(2)}) %collective-permute-start.34) | collective-permute-done | bytes 262176 | tf_op jit(solution)/shard_map/ppermute | solution.py:19
  167.7 0.6 slice_bitcast_fusion
  168.4 1.8 collective-permute-start.37
  170.3 0.4 collective-permute-start.36
  170.7 0.6 slice_bitcast_fusion.12
  171.3 1.8 collective-permute-start.13
  173.1 0.3 collective-permute-start.20
  173.5 1.3 collective-permute-done.36.refs_2_
  174.8 1.0 collective-permute-start.12
  175.9 0.6 copy-done.25
  176.5 2.3 %place.4.refs_4_ = bf16[256,2048]{1,0:T(8,128)(2,1)} custom-call(s32[6]{0:T(128)} %pad_add_fusion.place_ref, bf16[64,512]{1,0:T(8,128)(2,1)} %get-tuple-element.8.refs_0_, bf16[64,512]{1,0:T(8,128)(2,1)} %copy-done.25, bf16[64,512]{1,0:T(8,128)(2,1)} %copy-done.23, bf16[64,512]{1,0:T(8,128)(2,1)} %copy-done.22), custom_call_target="tpu_custom_call" | custom-call | bytes 524288 | tf_op jit(solution)/shard_map/place/pallas_call | solution.py:231
  178.8 2.3 %place.5.refs_4_ = bf16[256,2048]{1,0:T(8,128)(2,1)} custom-call(s32[6]{0:T(128)} %pad_add_fusion.place_ref, bf16[64,512]{1,0:T(8,128)(2,1)} %get-tuple-element.12.refs_0_, bf16[64,512]{1,0:T(8,128)(2,1)} %copy-done.20, bf16[64,512]{1,0:T(8,128)(2,1)} %copy-done.19, bf16[64,512]{1,0:T(8,128)(2,1)} %copy-done.18, ...), custom_call_target="tpu_custom_call", output_to_operand_aliasing={{}: (5, {})} | custom-call | bytes 524288 | tf_op jit(solution)/shard_map/place/pallas_call | solution.py:231
  181.2 0.6 copy-done.26
  181.8 2.3 %place.6.refs_4_ = bf16[256,2048]{1,0:T(8,128)(2,1)} custom-call(s32[6]{0:T(128)} %pad_add_fusion.place_ref, bf16[64,512]{1,0:T(8,128)(2,1)} %get-tuple-element.16.refs_0_, bf16[64,512]{1,0:T(8,128)(2,1)} %copy-done.28, bf16[64,512]{1,0:T(8,128)(2,1)} %copy-done.26, bf16[64,512]{1,0:T(8,128)(2,1)} %copy-done.17, ...), custom_call_target="tpu_custom_call", output_to_operand_aliasing={{}: (5, {})} | custom-call | bytes 524288 | tf_op jit(solution)/shard_map/place/pallas_call | solution.py:231
  184.2 0.6 copy-done.21
  184.8 2.3 %place.7 = bf16[256,2048]{1,0:T(8,128)(2,1)} custom-call(s32[6]{0:T(128)} %pad_add_fusion.place_ref, bf16[64,512]{1,0:T(8,128)(2,1)} %get-tuple-element.20.refs_0_, bf16[64,512]{1,0:T(8,128)(2,1)} %copy-done.27, bf16[64,512]{1,0:T(8,128)(2,1)} %copy-done.24, bf16[64,512]{1,0:T(8,128)(2,1)} %copy-done.21, ...), custom_call_target="tpu_custom_call", output_to_operand_aliasing={{}: (5, {})} | custom-call | bytes 524288 | tf_op jit(solution)/shard_map/place/pallas_call | solution.py:231
  (119 shorter events, 1.7 us)
Async XLA Ops:
  0.0 10.3 %collective-permute-start.2 = (bf16[2,256,256]{2,1,0:T(8,128)(2,1)}, bf16[2,256,256]{2,1,0:T(8,128)(2,1)S(1)}, u32[]{:S(2)}, u32[]{:S(2)}) collective-permute-start(bf16[2,256,256]{2,1,0:T(8,128)(2,1)} %param.9), channel_id=1, source_target_pairs={{0,8},{4,12},{8,0},{12,4},{1,9},{5,13},{9,1},{13,5},{2,10},{6,14},... | collective-permute-start | bytes 786440 | tf_op jit(solution)/shard_map/ppermute | solution.py:19
  3.0 12.1 %collective-permute-start.3 = (bf16[2,256,256]{2,1,0:T(8,128)(2,1)}, bf16[2,256,256]{2,1,0:T(8,128)(2,1)S(1)}, u32[]{:S(2)}, u32[]{:S(2)}) collective-permute-start(bf16[2,256,256]{2,1,0:T(8,128)(2,1)} %param.10), channel_id=1, source_target_pairs={{0,8},{4,12},{8,0},{12,4},{1,9},{5,13},{9,1},{13,5},{2,10},{6,14},... | collective-permute-start | bytes 786440 | tf_op jit(solution)/shard_map/ppermute | solution.py:19
  3.0 23.8 %collective-permute-start = (bf16[2,256,256]{2,1,0:T(8,128)(2,1)}, bf16[2,256,256]{2,1,0:T(8,128)(2,1)S(1)}, u32[]{:S(2)}, u32[]{:S(2)}) collective-permute-start(bf16[2,256,256]{2,1,0:T(8,128)(2,1)} %param.9), channel_id=1, source_target_pairs={{0,4},{4,0},{8,12},{12,8},{1,5},{5,1},{9,13},{13,9},{2,6},{6,2},{1... | collective-permute-start | bytes 786440 | tf_op jit(solution)/shard_map/ppermute | solution.py:19
  3.0 23.8 %collective-permute-start.1 = (bf16[2,256,256]{2,1,0:T(8,128)(2,1)}, bf16[2,256,256]{2,1,0:T(8,128)(2,1)S(1)}, u32[]{:S(2)}, u32[]{:S(2)}) collective-permute-start(bf16[2,256,256]{2,1,0:T(8,128)(2,1)} %param.10), channel_id=1, source_target_pairs={{0,4},{4,0},{8,12},{12,8},{1,5},{5,1},{9,13},{13,9},{2,6},{6,2},{1... | collective-permute-start | bytes 786440 | tf_op jit(solution)/shard_map/ppermute | solution.py:19
  10.3 15.8 %copy-start.29 = (bf16[2,256,256]{2,1,0:T(8,128)(2,1)}, bf16[2,256,256]{2,1,0:T(8,128)(2,1)S(1)}, u32[]{:S(2)}) copy-start(bf16[2,256,256]{2,1,0:T(8,128)(2,1)S(1)} %collective-permute-done.2) | copy-start | bytes 786436
  10.3 16.4 %collective-permute-start.4 = (bf16[2,256,256]{2,1,0:T(8,128)(2,1)S(1)}, bf16[2,256,256]{2,1,0:T(8,128)(2,1)S(1)}, u32[]{:S(2)}, u32[]{:S(2)}) collective-permute-start(bf16[2,256,256]{2,1,0:T(8,128)(2,1)S(1)} %collective-permute-done.2), channel_id=1, source_target_pairs={{0,4},{4,0},{8,12},{12,8},{1,5},{5,1},{9,13},{13,9},{2,6},{6,2},{1... | collective-permute-start | bytes 786440 | tf_op jit(solution)/shard_map/ppermute | solution.py:19
  15.1 11.0 %copy-start.30 = (bf16[2,256,256]{2,1,0:T(8,128)(2,1)}, bf16[2,256,256]{2,1,0:T(8,128)(2,1)S(1)}, u32[]{:S(2)}) copy-start(bf16[2,256,256]{2,1,0:T(8,128)(2,1)S(1)} %collective-permute-done.3) | copy-start | bytes 786436
  15.1 11.7 %collective-permute-start.5 = (bf16[2,256,256]{2,1,0:T(8,128)(2,1)S(1)}, bf16[2,256,256]{2,1,0:T(8,128)(2,1)S(1)}, u32[]{:S(2)}, u32[]{:S(2)}) collective-permute-start(bf16[2,256,256]{2,1,0:T(8,128)(2,1)S(1)} %collective-permute-done.3), channel_id=1, source_target_pairs={{0,4},{4,0},{8,12},{12,8},{1,5},{5,1},{9,13},{13,9},{2,6},{6,2},{1... | collective-permute-start | bytes 786440 | tf_op jit(solution)/shard_map/ppermute | solution.py:19
  26.8 0.7 copy-start.31
  26.8 0.8 copy-start.32
  26.8 0.8 copy-start.33
  26.8 0.9 copy-start.34
  32.3 14.5 %copy-start.4 = (bf16[64,2048]{1,0:T(8,128)(2,1)S(1)}, bf16[64,2048]{1,0:T(8,128)(2,1)}, u32[]{:S(2)}) copy-start(bf16[64,2048]{1,0:T(8,128)(2,1)} %messages.5.refs_0_) | copy-start | bytes 786436
  37.2 24.9 %collective-permute-start.7 = (bf16[64,2048]{1,0:T(8,128)(2,1)}, bf16[64,2048]{1,0:T(8,128)(2,1)S(1)}, u32[]{:S(2)}, u32[]{:S(2)}) collective-permute-start(bf16[64,2048]{1,0:T(8,128)(2,1)} %messages.4.refs_0_), channel_id=1, source_target_pairs={{0,8},{4,12},{8,0},{12,4},{1,9},{5,13},{9,1},{13,5},{2,10},{6,14},... | collective-permute-start | bytes 786440 | tf_op jit(solution)/shard_map/ppermute | solution.py:19
  46.6 19.5 %collective-permute-start.6 = (bf16[64,2048]{1,0:T(8,128)(2,1)}, bf16[64,2048]{1,0:T(8,128)(2,1)S(1)}, u32[]{:S(2)}, u32[]{:S(2)}) collective-permute-start(bf16[64,2048]{1,0:T(8,128)(2,1)} %messages.4.refs_0_), channel_id=1, source_target_pairs={{0,4},{4,0},{8,12},{12,8},{1,5},{5,1},{9,13},{13,9},{2,6},{6,2},{1... | collective-permute-start | bytes 786440 | tf_op jit(solution)/shard_map/ppermute | solution.py:19
  46.7 19.5 %collective-permute-start.15 = (bf16[64,2048]{1,0:T(8,128)(2,1)S(1)}, bf16[64,2048]{1,0:T(8,128)(2,1)S(1)}, u32[]{:S(2)}, u32[]{:S(2)}) collective-permute-start(bf16[64,2048]{1,0:T(8,128)(2,1)S(1)} %copy-done.4), channel_id=1, source_target_pairs={{0,8},{4,12},{8,0},{12,4},{1,9},{5,13},{9,1},{13,5},{2,10},{6,14},... | collective-permute-start | bytes 786440 | tf_op jit(solution)/shard_map/ppermute | solution.py:19
  47.1 19.6 %collective-permute-start.14 = (bf16[64,2048]{1,0:T(8,128)(2,1)S(1)}, bf16[64,2048]{1,0:T(8,128)(2,1)S(1)}, u32[]{:S(2)}, u32[]{:S(2)}) collective-permute-start(bf16[64,2048]{1,0:T(8,128)(2,1)S(1)} %copy-done.4), channel_id=1, source_target_pairs={{0,4},{4,0},{8,12},{12,8},{1,5},{5,1},{9,13},{13,9},{2,6},{6,2},{1... | collective-permute-start | bytes 786440 | tf_op jit(solution)/shard_map/ppermute | solution.py:19
  51.7 14.5 %copy-start.8 = (bf16[64,2048]{1,0:T(8,128)(2,1)S(1)}, bf16[64,2048]{1,0:T(8,128)(2,1)}, u32[]{:S(2)}) copy-start(bf16[64,2048]{1,0:T(8,128)(2,1)} %messages.6.refs_0_) | copy-start | bytes 786436
  51.7 15.1 %collective-permute-start.23 = (bf16[64,2048]{1,0:T(8,128)(2,1)}, bf16[64,2048]{1,0:T(8,128)(2,1)S(1)}, u32[]{:S(2)}, u32[]{:S(2)}) collective-permute-start(bf16[64,2048]{1,0:T(8,128)(2,1)} %messages.6.refs_0_), channel_id=1, source_target_pairs={{0,8},{4,12},{8,0},{12,4},{1,9},{5,13},{9,1},{13,5},{2,10},{6,14},... | collective-permute-start | bytes 786440 | tf_op jit(solution)/shard_map/ppermute | solution.py:19
  62.1 11.6 %copy-start.3 = (bf16[64,2048]{1,0:T(8,128)(2,1)}, bf16[64,2048]{1,0:T(8,128)(2,1)S(1)}, u32[]{:S(2)}) copy-start(bf16[64,2048]{1,0:T(8,128)(2,1)S(1)} %collective-permute-done.7.refs_2_) | copy-start | bytes 786436
  62.1 11.1 %collective-permute-start.31 = (bf16[64,2048]{1,0:T(8,128)(2,1)}, bf16[64,2048]{1,0:T(8,128)(2,1)S(1)}, u32[]{:S(2)}, u32[]{:S(2)}) collective-permute-start(bf16[64,2048]{1,0:T(8,128)(2,1)} %messages.7.refs_0_), channel_id=1, source_target_pairs={{0,8},{4,12},{8,0},{12,4},{1,9},{5,13},{9,1},{13,5},{2,10},{6,14},... | collective-permute-start | bytes 786440 | tf_op jit(solution)/shard_map/ppermute | solution.py:19
  66.1 7.7 %copy-start.5 = (bf16[64,2048]{1,0:T(8,128)(2,1)}, bf16[64,2048]{1,0:T(8,128)(2,1)S(1)}, u32[]{:S(2)}) copy-start(bf16[64,2048]{1,0:T(8,128)(2,1)S(1)} %collective-permute-done.6.refs_1_) | copy-start | bytes 786436
  66.1 7.3 %collective-permute-start.8 = (bf16[64,2048]{1,0:T(8,128)(2,1)S(1)}, bf16[64,2048]{1,0:T(8,128)(2,1)S(1)}, u32[]{:S(2)}, u32[]{:S(2)}) collective-permute-start(bf16[64,2048]{1,0:T(8,128)(2,1)S(1)} %collective-permute-done.7.refs_2_), channel_id=1, source_target_pairs={{0,4},{4,0},{8,12},{12,8},{1,5},{5,1},{9,13},{13,9},{2,6},{6,2},{1... | collective-permute-start | bytes 786440 | tf_op jit(solution)/shard_map/ppermute | solution.py:19
  66.2 12.5 %copy-start.6 = (bf16[64,2048]{1,0:T(8,128)(2,1)}, bf16[64,2048]{1,0:T(8,128)(2,1)S(1)}, u32[]{:S(2)}) copy-start(bf16[64,2048]{1,0:T(8,128)(2,1)S(1)} %collective-permute-done.15.refs_2_) | copy-start | bytes 786436
  66.2 18.8 %collective-permute-start.22 = (bf16[64,2048]{1,0:T(8,128)(2,1)S(1)}, bf16[64,2048]{1,0:T(8,128)(2,1)S(1)}, u32[]{:S(2)}, u32[]{:S(2)}) collective-permute-start(bf16[64,2048]{1,0:T(8,128)(2,1)S(1)} %copy-done.8), channel_id=1, source_target_pairs={{0,4},{4,0},{8,12},{12,8},{1,5},{5,1},{9,13},{13,9},{2,6},{6,2},{1... | collective-permute-start | bytes 786440 | tf_op jit(solution)/shard_map/ppermute | solution.py:19
  66.7 12.1 %copy-start.7 = (bf16[64,2048]{1,0:T(8,128)(2,1)}, bf16[64,2048]{1,0:T(8,128)(2,1)S(1)}, u32[]{:S(2)}) copy-start(bf16[64,2048]{1,0:T(8,128)(2,1)S(1)} %collective-permute-done.14.refs_1_) | copy-start | bytes 786436
  66.7 12.1 %collective-permute-start.16 = (bf16[64,2048]{1,0:T(8,128)(2,1)S(1)}, bf16[64,2048]{1,0:T(8,128)(2,1)S(1)}, u32[]{:S(2)}, u32[]{:S(2)}) collective-permute-start(bf16[64,2048]{1,0:T(8,128)(2,1)S(1)} %collective-permute-done.15.refs_2_), channel_id=1, source_target_pairs={{0,4},{4,0},{8,12},{12,8},{1,5},{5,1},{9,13},{13,9},{2,6},{6,2},{1... | collective-permute-start | bytes 786440 | tf_op jit(solution)/shard_map/ppermute | solution.py:19
  66.8 11.9 %copy-start.9 = (bf16[64,2048]{1,0:T(8,128)(2,1)}, bf16[64,2048]{1,0:T(8,128)(2,1)S(1)}, u32[]{:S(2)}) copy-start(bf16[64,2048]{1,0:T(8,128)(2,1)S(1)} %collective-permute-done.23.refs_2_) | copy-start | bytes 786436
  66.8 19.0 %collective-permute-start.24 = (bf16[64,2048]{1,0:T(8,128)(2,1)S(1)}, bf16[64,2048]{1,0:T(8,128)(2,1)S(1)}, u32[]{:S(2)}, u32[]{:S(2)}) collective-permute-start(bf16[64,2048]{1,0:T(8,128)(2,1)S(1)} %collective-permute-done.23.refs_2_), channel_id=1, source_target_pairs={{0,4},{4,0},{8,12},{12,8},{1,5},{5,1},{9,13},{13,9},{2,6},{6,2},{1... | collective-permute-start | bytes 786440 | tf_op jit(solution)/shard_map/ppermute | solution.py:19
  73.2 17.9 %copy-start.11 = (bf16[64,2048]{1,0:T(8,128)(2,1)}, bf16[64,2048]{1,0:T(8,128)(2,1)S(1)}, u32[]{:S(2)}) copy-start(bf16[64,2048]{1,0:T(8,128)(2,1)S(1)} %collective-permute-done.31.refs_2_) | copy-start | bytes 786436
  73.2 19.3 %collective-permute-start.30 = (bf16[64,2048]{1,0:T(8,128)(2,1)}, bf16[64,2048]{1,0:T(8,128)(2,1)S(1)}, u32[]{:S(2)}, u32[]{:S(2)}) collective-permute-start(bf16[64,2048]{1,0:T(8,128)(2,1)} %messages.7.refs_0_), channel_id=1, source_target_pairs={{0,4},{4,0},{8,12},{12,8},{1,5},{5,1},{9,13},{13,9},{2,6},{6,2},{1... | collective-permute-start | bytes 786440 | tf_op jit(solution)/shard_map/ppermute | solution.py:19
  73.3 0.7 copy-start.10
  73.3 19.2 %collective-permute-start.32 = (bf16[64,2048]{1,0:T(8,128)(2,1)S(1)}, bf16[64,2048]{1,0:T(8,128)(2,1)S(1)}, u32[]{:S(2)}, u32[]{:S(2)}) collective-permute-start(bf16[64,2048]{1,0:T(8,128)(2,1)S(1)} %collective-permute-done.31.refs_2_), channel_id=1, source_target_pairs={{0,4},{4,0},{8,12},{12,8},{1,5},{5,1},{9,13},{13,9},{2,6},{6,2},{1... | collective-permute-start | bytes 786440 | tf_op jit(solution)/shard_map/ppermute | solution.py:19
  78.7 1.7 copy-start.13
  78.7 39.3 %collective-permute-start.9 = (bf16[2,256,512]{2,1,0:T(8,128)(2,1)}, bf16[2,256,512]{2,1,0:T(8,128)(2,1)}, u32[]{:S(2)}, u32[]{:S(2)}) collective-permute-start(bf16[2,256,512]{2,1,0:T(8,128)(2,1)} %project.9), channel_id=1, source_target_pairs={{0,1},{1,0},{2,3},{3,2},{4,5},{5,4},{6,7},{7,6},{8,9},{9,8},{10,11... | collective-permute-start | bytes 1572872 | tf_op jit(solution)/shard_map/ppermute | solution.py:19
  85.1 0.7 copy-start.12
  85.1 37.1 %collective-permute-start.17 = (bf16[2,256,512]{2,1,0:T(8,128)(2,1)}, bf16[2,256,512]{2,1,0:T(8,128)(2,1)S(1)}, u32[]{:S(2)}, u32[]{:S(2)}) collective-permute-start(bf16[2,256,512]{2,1,0:T(8,128)(2,1)} %project.11), channel_id=1, source_target_pairs={{0,1},{1,0},{2,3},{3,2},{4,5},{5,4},{6,7},{7,6},{8,9},{9,8},{10,11... | collective-permute-start | bytes 1572872 | tf_op jit(solution)/shard_map/ppermute | solution.py:19
  91.1 31.7 %collective-permute-start.25 = (bf16[2,256,512]{2,1,0:T(8,128)(2,1)}, bf16[2,256,512]{2,1,0:T(8,128)(2,1)S(1)}, u32[]{:S(2)}, u32[]{:S(2)}) collective-permute-start(bf16[2,256,512]{2,1,0:T(8,128)(2,1)} %project.13), channel_id=1, source_target_pairs={{0,1},{1,0},{2,3},{3,2},{4,5},{5,4},{6,7},{7,6},{8,9},{9,8},{10,11... | collective-permute-start | bytes 1572872 | tf_op jit(solution)/shard_map/ppermute | solution.py:19
  98.6 34.7 %collective-permute-start.33 = (bf16[2,256,512]{2,1,0:T(8,128)(2,1)}, bf16[2,256,512]{2,1,0:T(8,128)(2,1)S(1)}, u32[]{:S(2)}, u32[]{:S(2)}) collective-permute-start(bf16[2,256,512]{2,1,0:T(8,128)(2,1)} %project.15), channel_id=1, source_target_pairs={{0,1},{1,0},{2,3},{3,2},{4,5},{5,4},{6,7},{7,6},{8,9},{9,8},{10,11... | collective-permute-start | bytes 1572872 | tf_op jit(solution)/shard_map/ppermute | solution.py:19
  113.2 8.9 %copy-start.2 = (bf16[2,256,512]{2,1,0:T(8,128)(2,1)S(1)}, bf16[2,256,512]{2,1,0:T(8,128)(2,1)}, u32[]{:S(2)}) copy-start(bf16[2,256,512]{2,1,0:T(8,128)(2,1)} %project.10) | copy-start | bytes 1572868
  118.0 4.8 %copy-start.1 = (bf16[2,256,512]{2,1,0:T(8,128)(2,1)S(1)}, bf16[2,256,512]{2,1,0:T(8,128)(2,1)}, u32[]{:S(2)}) copy-start(bf16[2,256,512]{2,1,0:T(8,128)(2,1)} %project.12) | copy-start | bytes 1572868
  118.0 15.3 %copy-start = (bf16[2,256,512]{2,1,0:T(8,128)(2,1)S(1)}, bf16[2,256,512]{2,1,0:T(8,128)(2,1)}, u32[]{:S(2)}) copy-start(bf16[2,256,512]{2,1,0:T(8,128)(2,1)} %project.14) | copy-start | bytes 1572868
  119.5 48.8 %collective-permute-start.10 = (bf16[1,256,512]{2,1,0:T(8,128)(2,1)S(1)}, bf16[1,256,512]{2,1,0:T(8,128)(2,1)S(1)}, u32[]{:S(2)}, u32[]{:S(2)}) collective-permute-start(bf16[1,256,512]{2,1,0:T(8,128)(2,1)S(1)} %slice.259), channel_id=1, source_target_pairs={{0,2},{1,3},{2,0},{3,1},{4,6},{5,7},{6,4},{7,5},{8,10},{9,11},{10,... | collective-permute-start | bytes 786440 | tf_op jit(solution)/shard_map/ppermute | solution.py:19
  122.4 35.4 %collective-permute-start.18 = (bf16[1,256,512]{2,1,0:T(8,128)(2,1)S(1)}, bf16[1,256,512]{2,1,0:T(8,128)(2,1)S(1)}, u32[]{:S(2)}, u32[]{:S(2)}) collective-permute-start(bf16[1,256,512]{2,1,0:T(8,128)(2,1)S(1)} %slice.258), channel_id=1, source_target_pairs={{0,2},{1,3},{2,0},{3,1},{4,6},{5,7},{6,4},{7,5},{8,10},{9,11},{10,... | collective-permute-start | bytes 786440 | tf_op jit(solution)/shard_map/ppermute | solution.py:19
  123.0 40.4 %collective-permute-start.26 = (bf16[1,256,512]{2,1,0:T(8,128)(2,1)S(1)}, bf16[1,256,512]{2,1,0:T(8,128)(2,1)S(1)}, u32[]{:S(2)}, u32[]{:S(2)}) collective-permute-start(bf16[1,256,512]{2,1,0:T(8,128)(2,1)S(1)} %slice.257), channel_id=1, source_target_pairs={{0,2},{1,3},{2,0},{3,1},{4,6},{5,7},{6,4},{7,5},{8,10},{9,11},{10,... | collective-permute-start | bytes 786440 | tf_op jit(solution)/shard_map/ppermute | solution.py:19
  133.5 34.1 %collective-permute-start.34 = (bf16[1,256,512]{2,1,0:T(8,128)(2,1)S(1)}, bf16[1,256,512]{2,1,0:T(8,128)(2,1)S(1)}, u32[]{:S(2)}, u32[]{:S(2)}) collective-permute-start(bf16[1,256,512]{2,1,0:T(8,128)(2,1)S(1)} %slice.256), channel_id=1, source_target_pairs={{0,2},{1,3},{2,0},{3,1},{4,6},{5,7},{6,4},{7,5},{8,10},{9,11},{10,... | collective-permute-start | bytes 786440 | tf_op jit(solution)/shard_map/ppermute | solution.py:19
  158.5 11.8 %collective-permute-start.21 = (bf16[64,512]{1,0:T(8,128)(2,1)S(1)}, bf16[64,512]{1,0:T(8,128)(2,1)S(1)}, u32[]{:S(2)}, u32[]{:S(2)}) collective-permute-start(bf16[64,512]{1,0:T(8,128)(2,1)S(1)} %get-tuple-element.13), channel_id=1, source_target_pairs={{0,12},{4,8},{8,4},{12,0},{1,13},{5,9},{9,5},{13,1},{2,14},{6,10},... | collective-permute-start | bytes 196616 | tf_op jit(solution)/shard_map/ppermute | solution.py:19
  164.1 6.6 %collective-permute-start.29 = (bf16[64,512]{1,0:T(8,128)(2,1)S(1)}, bf16[64,512]{1,0:T(8,128)(2,1)S(1)}, u32[]{:S(2)}, u32[]{:S(2)}) collective-permute-start(bf16[64,512]{1,0:T(8,128)(2,1)S(1)} %get-tuple-element.9), channel_id=1, source_target_pairs={{0,12},{4,8},{8,4},{12,0},{1,13},{5,9},{9,5},{13,1},{2,14},{6,10},... | collective-permute-start | bytes 196616 | tf_op jit(solution)/shard_map/ppermute | solution.py:19
  164.1 7.2 %collective-permute-start.28 = (bf16[64,512]{1,0:T(8,128)(2,1)S(1)}, bf16[64,512]{1,0:T(8,128)(2,1)S(1)}, u32[]{:S(2)}, u32[]{:S(2)}) collective-permute-start(bf16[64,512]{1,0:T(8,128)(2,1)S(1)} %get-tuple-element.10), channel_id=1, source_target_pairs={{0,8},{4,12},{8,0},{12,4},{1,9},{5,13},{9,1},{13,5},{2,10},{6,14},... | collective-permute-start | bytes 196616 | tf_op jit(solution)/shard_map/ppermute | solution.py:19
  167.6 5.5 %collective-permute-start.27 = (bf16[64,512]{1,0:T(8,128)(2,1)S(1)}, bf16[64,512]{1,0:T(8,128)(2,1)S(1)}, u32[]{:S(2)}, u32[]{:S(2)}) collective-permute-start(bf16[64,512]{1,0:T(8,128)(2,1)S(1)} %get-tuple-element.11), channel_id=1, source_target_pairs={{0,4},{4,0},{8,12},{12,8},{1,5},{5,1},{9,13},{13,9},{2,6},{6,2},{1... | collective-permute-start | bytes 196616 | tf_op jit(solution)/shard_map/ppermute | solution.py:19
  168.4 5.1 %collective-permute-start.37 = (bf16[64,512]{1,0:T(8,128)(2,1)S(1)}, bf16[64,512]{1,0:T(8,128)(2,1)S(1)}, u32[]{:S(2)}, u32[]{:S(2)}) collective-permute-start(bf16[64,512]{1,0:T(8,128)(2,1)S(1)} %get-tuple-element.5), channel_id=1, source_target_pairs={{0,12},{4,8},{8,4},{12,0},{1,13},{5,9},{9,5},{13,1},{2,14},{6,10},... | collective-permute-start | bytes 196616 | tf_op jit(solution)/shard_map/ppermute | solution.py:19
  170.3 10.9 %copy-start.17 = (bf16[64,512]{1,0:T(8,128)(2,1)}, bf16[64,512]{1,0:T(8,128)(2,1)S(1)}, u32[]{:S(2)}) copy-start(bf16[64,512]{1,0:T(8,128)(2,1)S(1)} %collective-permute-done.21.refs_3_) | copy-start | bytes 196612
  170.3 4.5 %collective-permute-start.36 = (bf16[64,512]{1,0:T(8,128)(2,1)S(1)}, bf16[64,512]{1,0:T(8,128)(2,1)S(1)}, u32[]{:S(2)}, u32[]{:S(2)}) collective-permute-start(bf16[64,512]{1,0:T(8,128)(2,1)S(1)} %get-tuple-element.6), channel_id=1, source_target_pairs={{0,8},{4,12},{8,0},{12,4},{1,9},{5,13},{9,1},{13,5},{2,10},{6,14},... | collective-permute-start | bytes 196616 | tf_op jit(solution)/shard_map/ppermute | solution.py:19
  170.7 8.1 %copy-start.18 = (bf16[64,512]{1,0:T(8,128)(2,1)}, bf16[64,512]{1,0:T(8,128)(2,1)S(1)}, u32[]{:S(2)}) copy-start(bf16[64,512]{1,0:T(8,128)(2,1)S(1)} %collective-permute-done.29.refs_3_) | copy-start | bytes 196612
  170.7 5.2 %collective-permute-start.35 = (bf16[64,512]{1,0:T(8,128)(2,1)S(1)}, bf16[64,512]{1,0:T(8,128)(2,1)S(1)}, u32[]{:S(2)}, u32[]{:S(2)}) collective-permute-start(bf16[64,512]{1,0:T(8,128)(2,1)S(1)} %get-tuple-element.7), channel_id=1, source_target_pairs={{0,4},{4,0},{8,12},{12,8},{1,5},{5,1},{9,13},{13,9},{2,6},{6,2},{1... | collective-permute-start | bytes 196616 | tf_op jit(solution)/shard_map/ppermute | solution.py:19
  171.3 7.5 %copy-start.19 = (bf16[64,512]{1,0:T(8,128)(2,1)}, bf16[64,512]{1,0:T(8,128)(2,1)S(1)}, u32[]{:S(2)}) copy-start(bf16[64,512]{1,0:T(8,128)(2,1)S(1)} %collective-permute-done.28.refs_2_) | copy-start | bytes 196612
  171.3 12.8 %collective-permute-start.13 = (bf16[64,512]{1,0:T(8,128)(2,1)S(1)}, bf16[64,512]{1,0:T(8,128)(2,1)S(1)}, u32[]{:S(2)}, u32[]{:S(2)}) collective-permute-start(bf16[64,512]{1,0:T(8,128)(2,1)S(1)} %get-tuple-element.17), channel_id=1, source_target_pairs={{0,12},{4,8},{8,4},{12,0},{1,13},{5,9},{9,5},{13,1},{2,14},{6,10},... | collective-permute-start | bytes 196616 | tf_op jit(solution)/shard_map/ppermute | solution.py:19
  173.1 5.7 %copy-start.20 = (bf16[64,512]{1,0:T(8,128)(2,1)}, bf16[64,512]{1,0:T(8,128)(2,1)S(1)}, u32[]{:S(2)}) copy-start(bf16[64,512]{1,0:T(8,128)(2,1)S(1)} %collective-permute-done.27.refs_1_) | copy-start | bytes 196612
  173.1 8.0 %collective-permute-start.20 = (bf16[64,512]{1,0:T(8,128)(2,1)S(1)}, bf16[64,512]{1,0:T(8,128)(2,1)S(1)}, u32[]{:S(2)}, u32[]{:S(2)}) collective-permute-start(bf16[64,512]{1,0:T(8,128)(2,1)S(1)} %get-tuple-element.14), channel_id=1, source_target_pairs={{0,8},{4,12},{8,0},{12,4},{1,9},{5,13},{9,1},{13,5},{2,10},{6,14},... | collective-permute-start | bytes 196616 | tf_op jit(solution)/shard_map/ppermute | solution.py:19
  173.5 2.4 %copy-start.22 = (bf16[64,512]{1,0:T(8,128)(2,1)}, bf16[64,512]{1,0:T(8,128)(2,1)S(1)}, u32[]{:S(2)}) copy-start(bf16[64,512]{1,0:T(8,128)(2,1)S(1)} %collective-permute-done.37.refs_3_) | copy-start | bytes 196612
  173.5 7.7 %collective-permute-start.19 = (bf16[64,512]{1,0:T(8,128)(2,1)S(1)}, bf16[64,512]{1,0:T(8,128)(2,1)S(1)}, u32[]{:S(2)}, u32[]{:S(2)}) collective-permute-start(bf16[64,512]{1,0:T(8,128)(2,1)S(1)} %get-tuple-element.15), channel_id=1, source_target_pairs={{0,4},{4,0},{8,12},{12,8},{1,5},{5,1},{9,13},{13,9},{2,6},{6,2},{1... | collective-permute-start | bytes 196616 | tf_op jit(solution)/shard_map/ppermute | solution.py:19
  174.8 1.1 copy-start.23
  174.8 9.3 %collective-permute-start.12 = (bf16[64,512]{1,0:T(8,128)(2,1)S(1)}, bf16[64,512]{1,0:T(8,128)(2,1)S(1)}, u32[]{:S(2)}, u32[]{:S(2)}) collective-permute-start(bf16[64,512]{1,0:T(8,128)(2,1)S(1)} %get-tuple-element.18), channel_id=1, source_target_pairs={{0,8},{4,12},{8,0},{12,4},{1,9},{5,13},{9,1},{13,5},{2,10},{6,14},... | collective-permute-start | bytes 196616 | tf_op jit(solution)/shard_map/ppermute | solution.py:19
  175.9 8.3 %collective-permute-start.11 = (bf16[64,512]{1,0:T(8,128)(2,1)S(1)}, bf16[64,512]{1,0:T(8,128)(2,1)S(1)}, u32[]{:S(2)}, u32[]{:S(2)}) collective-permute-start(bf16[64,512]{1,0:T(8,128)(2,1)S(1)} %get-tuple-element.19), channel_id=1, source_target_pairs={{0,4},{4,0},{8,12},{12,8},{1,5},{5,1},{9,13},{13,9},{2,6},{6,2},{1... | collective-permute-start | bytes 196616 | tf_op jit(solution)/shard_map/ppermute | solution.py:19
  (9 other events, 5.9 us)
